TPU v7x, 128 devices: a whole 4x4x4 slice. The times are simulated.
128 devices in a mesh: wide: 32 (over x, z, core), narrow: 4 (over y).
Axes of the slice: x: 4, y: 4, z: 4, core: 2. Of those that a mesh axis runs over, the one named last changes fastest.
Arguments:
- tokens: bfloat16 [262144, 1024], P(('wide', 'narrow')), may hold values from -64 to 64
- slot_params: bfloat16 [1024, 512], replicated, may hold values from -2.5 to 2.5
- expert_in: bfloat16 [128, 1024, 4096], P('wide', None, 'narrow'), may hold values from -0.1875 to 0.1875
- expert_out: bfloat16 [128, 4096, 1024], P('wide', 'narrow'), may hold values from -0.09375 to 0.09375
Outputs:
- mixed: bfloat16 [262144, 1024], P(('wide', 'narrow'))
All inputs are finite; a program needn't handle non-finite values.
Results may differ from a plain program's by a relative error of at most 0.0071.
Values may be sent and summed in bfloat16 or wider, within the bound.
A program may use at most 128 MiB of HBM per device.

v0:
```python
import jax
import jax.numpy as jnp
from jax import lax
from jax.sharding import PartitionSpec as P

SLOT_PER = 4


def divide_rows(summed, slot_totals):
    return (summed / slot_totals[:, None]).astype(jnp.bfloat16)


def shards(tokens, slot_params, expert_in, expert_out):
    logits = jnp.dot(tokens, slot_params, preferred_element_type=jnp.float32)
    local_peak = jnp.max(logits, axis=0)
    column_peak = lax.pmax(local_peak, ("wide", "narrow"))
    weights = jnp.exp(logits - column_peak)
    slot_totals = lax.psum(jnp.sum(weights, axis=0), ("wide", "narrow"))
    dispatch = weights.astype(jnp.bfloat16)
    slot_count = slot_params.shape[1]
    row_count = slot_count // lax.axis_size("wide")
    columns = dispatch
    partial_value = lax.psum_scatter(
        lax.dot_general(
            columns, tokens, (((0,), (0,)), ((), ())), preferred_element_type=jnp.float32
        ),
        "wide",
        scatter_dimension=0,
        tiled=True,
    )
    summed = lax.psum(partial_value, "narrow")
    owned_totals = lax.dynamic_slice_in_dim(
        slot_totals, lax.axis_index("wide") * row_count, row_count
    )
    slot_in = divide_rows(summed, owned_totals)
    slot_stack = slot_in.reshape(expert_in.shape[0], SLOT_PER, slot_in.shape[1])
    hidden = jax.nn.gelu(
        jnp.einsum("esd,edh->esh", slot_stack, expert_in, preferred_element_type=jnp.float32)
    ).astype(jnp.bfloat16)
    expert_sum = jnp.einsum("esh,ehd->esd", hidden, expert_out, preferred_element_type=jnp.float32)
    expert_sum = expert_sum.reshape(-1, expert_sum.shape[2])
    mixing = jax.nn.softmax(logits, axis=1).astype(jnp.bfloat16)
    whole_rows = lax.psum(expert_sum, "narrow").astype(jnp.bfloat16)
    columns = mixing
    mixed = jnp.dot(
        columns,
        lax.all_gather(whole_rows, "wide", axis=0, tiled=True),
        preferred_element_type=jnp.float32,
    )
    return mixed.astype(jnp.bfloat16)


def solution(mesh):
    return jax.shard_map(
        shards,
        mesh=mesh,
        in_specs=(
            P(("wide", "narrow"), None),
            P(),
            P("wide", None, "narrow"),
            P("wide", "narrow", None),
        ),
        out_specs=P(("wide", "narrow"), None),
        check_vma=False,
    )
```

profile of v0, /device:TPU:1, one launch (start us, length us, event | category | flops | bytes accessed | tf_op | source)
XLA Modules:
  0.0 312.3 jit_solution(13459068889585292751)
XLA Ops:
  6.5 0.0 copy-start
  6.5 0.0 reduce-scatter.2.cloned.1.call-start
  6.5 1.2 copy-done
  7.8 6.5 %fusion.26 = (f32[2048]{0:T(1024)S(1)}, f32[512]{0:T(512)S(1)}, f32[2048,512]{1,0:T(8,128)}) fusion(bf16[2048,1024]{1,0:T(8,128)(2,1)} %param.4, bf16[1024,512]{1,0:T(8,128)(2,1)S(1)} %copy-done), kind=kOutput, calls=%fused_computation.30 | convolution fusion | flops 2149578240 | bytes 9447424 | tf_op jit(solution)/shard_map/dot_general | solution.py:14
  14.2 68.6 %pmax.7 = f32[512]{0:T(512)S(1)} all-reduce(f32[512]{0:T(512)S(1)} %get-tuple-element.8), channel_id=1, replica_groups=mesh['wide'=32,'narrow'=4] {'wide','narrow'}, use_global_device_ids=true, to_apply=%region_3.0 | all-reduce | flops 512 | bytes 4096 | tf_op jit(solution)/shard_map/pmax | solution.py:16
  82.8 7.2 %fusion.3 = f32[512,1024]{1,0:T(8,128)} fusion(bf16[2048,1024]{1,0:T(8,128)(2,1)} %param.4, f32[2048,512]{1,0:T(8,128)} %get-tuple-element.9, f32[512]{0:T(512)S(1)} %pmax.7), kind=kOutput, calls=%fused_computation.7 | convolution fusion | flops 2149580800 | bytes 10487808 | tf_op jit(solution)/shard_map/dot_general | solution.py:24
  90.0 0.0 reduce-scatter.2.cloned.1.call-update
  90.0 0.0 all-reduce.2.cloned.1.call-start
  90.1 73.9 %reduce-scatter.2.cloned.1.call-done = f32[16,1024]{1,0:T(8,128)} async-done(((f32[512,1024]{1,0:T(8,128)}), f32[16,1024]{1,0:T(8,128)}) %reduce-scatter.2.cloned.1.call-update) | async-done | bytes 65552 | tf_op jit(solution)/shard_map/reduce_scatter | solution.py:23
  163.9 0.0 all-reduce.2.cloned.1.call-update
  164.0 0.0 all-gather.2.cloned.1.call-start
  164.0 3.1 %fusion = (f32[2048]{0:T(1024)S(1)}, f32[512]{0:T(512)S(1)}) fusion(f32[2048,512]{1,0:T(8,128)} %get-tuple-element.9, f32[2048]{0:T(1024)S(1)} %get-tuple-element.7, f32[512]{0:T(512)S(1)} %pmax.7), kind=kLoop, calls=%fused_computation.4 | loop fusion | flops 4191744 | bytes 4214784 | tf_op jit(solution)/shard_map/reduce_sum | solution.py:42
  167.2 66.0 %psum.22 = f32[512]{0:T(512)S(1)} all-reduce(f32[512]{0:T(512)S(1)} %get-tuple-element.6), channel_id=1, replica_groups=mesh['wide'=32,'narrow'=4] {'wide','narrow'}, use_global_device_ids=true, to_apply=%region_7.0 | all-reduce | flops 512 | bytes 4096 | tf_op jit(solution)/shard_map/psum | solution.py:18
  233.2 0.1 dynamic_slice.3
  233.3 0.0 all-reduce.2.cloned.1.call-done
  233.3 0.9 divide_convert_fusion.2
  234.2 8.0 %fusion.16 = f32[4,4,1024]{2,1,0:T(4,128)S(1)} fusion(bf16[4,1024,1024]{2,1,0:T(8,128)(2,1)} %param.7, bf16[4,4,1024]{2,1,0:T(4,128)(2,1)S(1)} %reshape.10, bf16[4,1024,1024]{2,1,0:T(8,128)(2,1)} %param.6), kind=kOutput, calls=%fused_computation.21 | convolution fusion | flops 67256320 | bytes 16875520 | tf_op jit(solution)/shard_map/esh,ehd->esd/dot_general | solution.py:40
  242.3 12.6 %psum.23 = bf16[16,1024]{1,0:T(8,128)(2,1)} all-reduce(f32[16,1024]{1,0:T(8,128)S(1)} %reshape.11), channel_id=1, replica_groups=mesh['wide'=32,'narrow'=4] {'narrow'}, use_global_device_ids=true, to_apply=%region_8.0 | all-reduce | flops 16384 | bytes 98304 | tf_op jit(solution)/shard_map/psum | solution.py:43
  254.9 0.0 all-gather.2.cloned.1.call-update
  254.9 43.9 %all-gather.2.cloned.1.call-done = bf16[512,1024]{1,0:T(8,128)(2,1)} async-done(((bf16[16,1024]{1,0:T(8,128)(2,1)}), bf16[512,1024]{1,0:T(8,128)(2,1)}) %all-gather.2.cloned.1.call-update) | async-done | bytes 1048592 | tf_op jit(solution)/shard_map/all_gather | solution.py:47
  298.7 7.0 %convolution_convert_fusion = bf16[2048,1024]{1,0:T(8,128)(2,1)} fusion(bf16[512,1024]{1,0:T(8,128)(2,1)} %all-gather.2.cloned.1.call-done, f32[2048,512]{1,0:T(8,128)} %get-tuple-element.9, f32[2048]{0:T(1024)S(1)} %get-tuple-element.5, f32[2048]{0:T(1024)S(1)} %get-tuple-element.7), kind=kOutput, calls=%fused_computation.3 | convolution fusion | flops 2152726528 | bytes 9453568 | tf_op jit(solution)/shard_map/dot_general | solution.py:45
  (2 shorter events, 0.1 us)
Async XLA Ops:
  6.5 1.2 copy-start
  6.5 157.4 %reduce-scatter.2.cloned.1.call-start = ((), (), s32[]{:S(2)}) async-start(), calls=%async_computation.1 | async-start | bytes 2162688 | tf_op jit(solution)/shard_map/reduce_scatter | solution.py:23
  90.0 143.2 %all-reduce.2.cloned.1.call-start = ((), (), s32[]{:S(2)}) async-start(), calls=%async_computation.2 | async-start | bytes 131072 | tf_op jit(solution)/shard_map/psum | solution.py:31
  164.0 134.8 %all-gather.2.cloned.1.call-start = ((), (), s32[]{:S(2)}) async-start(), calls=%async_computation.3 | async-start | bytes 1081344 | tf_op jit(solution)/shard_map/all_gather | solution.py:47
Sparse Core Ops, SparseCore 0:
  90.2 73.7 reduce-scatter.1
  166.2 40.1 all-reduce.1
  255.0 43.6 all-gather.1
where the time goes:
time: 313 us; the launch traced here: 312 us
  blocking collectives  147 us (47%)
  waiting for transfers between devices  118 us (38%)
  matrix products  28.7 us (9%)
  between operations  13.1 us (4%)
  other arithmetic  4.06 us (1%)
    reduce_scatter x1, waiting for transfers between devices, shards(): lax.psum_scatter(lax.dot_general(columns, tokens, (((0,), (0,)), ((), ())...  73.9 us
    pmax x1, blocking collectives, shards(): column_peak = lax.pmax(local_peak, ('wide', 'narrow'))  68.6 us
    psum x1, blocking collectives, shards(): slot_totals = lax.psum(jnp.sum(weights, axis=0), ('wide', 'narrow'))  66 us
    all_gather x1, waiting for transfers between devices, shards(): lax.all_gather(whole_rows, 'wide', axis=0, tiled=True)  43.9 us
    psum x1, blocking collectives, shards(): whole_rows = lax.psum(expert_sum, 'narrow').astype(jnp.bfloat16)  12.6 us
    dot_general x1, matrix products, shards(): jnp.einsum('esh,ehd->esd', hidden, expert_out, preferred_element_type=jnp...  8.04 us
    dot_general x1, matrix products, shards(): lax.dot_general(columns, tokens, (((0,), (0,)), ((), ())), preferred_elem...  7.15 us
    dot_general x1, matrix products, shards(): jnp.dot(columns, lax.all_gather(whole_rows, 'wide', axis=0, tiled=True),...  7.05 us
  transfers between devices with their start and end apart: 3, of which 2 were waited for; matrix products, arithmetic and copies ran while one was open for 1% of the time, Pallas kernels for 0%

commit v1 on v0

--- a/solution.py
+++ b/solution.py
@@ -4,6 +4,11 @@
 from jax.sharding import PartitionSpec as P
 
 SLOT_PER = 4
+
+
+def gather_by_exchange(x, axis, dim):
+    copies = jnp.concatenate([x] * lax.axis_size(axis), axis=dim)
+    return lax.all_to_all(copies, axis, dim, dim, tiled=True)
 
 
 def divide_rows(summed, slot_totals):
@@ -43,9 +48,7 @@
     whole_rows = lax.psum(expert_sum, "narrow").astype(jnp.bfloat16)
     columns = mixing
     mixed = jnp.dot(
-        columns,
-        lax.all_gather(whole_rows, "wide", axis=0, tiled=True),
-        preferred_element_type=jnp.float32,
+        columns, gather_by_exchange(whole_rows, "wide", 0), preferred_element_type=jnp.float32
     )
     return mixed.astype(jnp.bfloat16)
 

time: 313 us -> 292 us (0.933)
  waiting for transfers between devices: 118 us -> 73.9 us
  blocking collectives: 147 us -> 172 us
    all_gather x1 -> x0, waiting for transfers between devices: 43.9 us -> none  [shards(): lax.all_gather(whole_rows, 'wide', axis=0, tiled=True)]
    all_to_all x0 -> x1, blocking collectives: none -> 25.7 us  [gather_by_exchange(): return lax.all_to_all(copies, axis, dim, dim, tiled=True)]
  transfers between devices with their start and end apart: 3 -> 2, of which waited for: 2 -> 1; matrix products, arithmetic and copies ran while one was open for 1% -> 1% of each run, Pallas kernels for 0% -> 0%
where the time goes in v1:
time: 292 us; the launch traced here: 291 us
  blocking collectives  172 us (59%)
  waiting for transfers between devices  73.9 us (25%)
  matrix products  25.9 us (9%)
  between operations  13.7 us (5%)
  other arithmetic  4.06 us (1%)
    reduce_scatter x1, waiting for transfers between devices, shards(): lax.psum_scatter(lax.dot_general(columns, tokens, (((0,), (0,)), ((), ())...  73.9 us
    pmax x1, blocking collectives, shards(): column_peak = lax.pmax(local_peak, ('wide', 'narrow'))  68.6 us
    psum x1, blocking collectives, shards(): slot_totals = lax.psum(jnp.sum(weights, axis=0), ('wide', 'narrow'))  66 us
    all_to_all x1, blocking collectives, gather_by_exchange(): return lax.all_to_all(copies, axis, dim, dim, tiled=True)  25.7 us
    psum x1, blocking collectives, shards(): whole_rows = lax.psum(expert_sum, 'narrow').astype(jnp.bfloat16)  11.8 us
    dot_general x1, matrix products, shards(): jnp.einsum('esh,ehd->esd', hidden, expert_out, preferred_element_type=jnp...  8.04 us
    dot_general x1, matrix products, shards(): lax.dot_general(columns, tokens, (((0,), (0,)), ((), ())), preferred_elem...  7.19 us
    dot_general x1, matrix products, shards(): logits = jnp.dot(tokens, slot_params, preferred_element_type=jnp.float32)  6.55 us
  transfers between devices with their start and end apart: 2, of which 1 were waited for; matrix products, arithmetic and copies ran while one was open for 1% of the time, Pallas kernels for 0%

profile of v1, /device:TPU:1, one launch (start us, length us, event | category | flops | bytes accessed | tf_op | source)
XLA Modules:
  0.0 291.1 jit_solution(18299405933131504033)
XLA Ops:
  6.5 0.0 copy-start
  6.5 0.0 reduce-scatter.2.cloned.1.call-start
  6.5 1.2 copy-done
  7.8 6.5 %fusion.26 = (f32[2048]{0:T(1024)S(1)}, f32[512]{0:T(512)S(1)}, f32[2048,512]{1,0:T(8,128)}) fusion(bf16[2048,1024]{1,0:T(8,128)(2,1)} %param.4, bf16[1024,512]{1,0:T(8,128)(2,1)S(1)} %copy-done), kind=kOutput, calls=%fused_computation.62 | convolution fusion | flops 2149578240 | bytes 9447424 | tf_op jit(solution)/shard_map/dot_general | solution.py:19
  14.3 68.6 %pmax.7 = f32[512]{0:T(512)S(1)} all-reduce(f32[512]{0:T(512)S(1)} %get-tuple-element.8), channel_id=1, replica_groups=mesh['wide'=32,'narrow'=4] {'wide','narrow'}, use_global_device_ids=true, to_apply=%region_3.0 | all-reduce | flops 512 | bytes 4096 | tf_op jit(solution)/shard_map/pmax | solution.py:21
  82.9 7.2 %fusion.3 = f32[512,1024]{1,0:T(8,128)} fusion(bf16[2048,1024]{1,0:T(8,128)(2,1)} %param.4, f32[2048,512]{1,0:T(8,128)} %get-tuple-element.9, f32[512]{0:T(512)S(1)} %pmax.7), kind=kOutput, calls=%fused_computation.7 | convolution fusion | flops 2149580800 | bytes 10487808 | tf_op jit(solution)/shard_map/dot_general | solution.py:29
  90.1 0.0 reduce-scatter.2.cloned.1.call-update
  90.2 0.0 all-reduce.2.cloned.1.call-start
  90.2 73.9 %reduce-scatter.2.cloned.1.call-done = f32[16,1024]{1,0:T(8,128)} async-done(((f32[512,1024]{1,0:T(8,128)}), f32[16,1024]{1,0:T(8,128)}) %reduce-scatter.2.cloned.1.call-update) | async-done | bytes 65552 | tf_op jit(solution)/shard_map/reduce_scatter | solution.py:28
  164.1 0.0 all-reduce.2.cloned.1.call-update
  164.1 3.1 %fusion = (f32[2048]{0:T(1024)S(1)}, f32[512]{0:T(512)S(1)}) fusion(f32[2048,512]{1,0:T(8,128)} %get-tuple-element.9, f32[2048]{0:T(1024)S(1)} %get-tuple-element.7, f32[512]{0:T(512)S(1)} %pmax.7), kind=kLoop, calls=%fused_computation.4 | loop fusion | flops 4191744 | bytes 4214784 | tf_op jit(solution)/shard_map/reduce_sum | solution.py:47
  167.3 66.0 %psum.22 = f32[512]{0:T(512)S(1)} all-reduce(f32[512]{0:T(512)S(1)} %get-tuple-element.6), channel_id=1, replica_groups=mesh['wide'=32,'narrow'=4] {'wide','narrow'}, use_global_device_ids=true, to_apply=%region_7.0 | all-reduce | flops 512 | bytes 4096 | tf_op jit(solution)/shard_map/psum | solution.py:23
  233.2 0.1 dynamic_slice.3
  233.3 0.0 all-reduce.2.cloned.1.call-done
  233.3 0.9 divide_convert_fusion.2
  234.3 8.0 %fusion.16 = f32[4,4,1024]{2,1,0:T(4,128)S(1)} fusion(bf16[4,1024,1024]{2,1,0:T(8,128)(2,1)} %param.7, bf16[4,4,1024]{2,1,0:T(4,128)(2,1)S(1)} %reshape.12, bf16[4,1024,1024]{2,1,0:T(8,128)(2,1)} %param.6), kind=kOutput, calls=%fused_computation.53 | convolution fusion | flops 67256320 | bytes 16875520 | tf_op jit(solution)/shard_map/esh,ehd->esd/dot_general | solution.py:45
  242.3 11.8 %psum.23 = bf16[16,1024]{1,0:T(8,128)(2,1)S(1)} all-reduce(f32[16,1024]{1,0:T(8,128)S(1)} %reshape.13), channel_id=1, replica_groups=mesh['wide'=32,'narrow'=4] {'narrow'}, use_global_device_ids=true, to_apply=%region_8.0 | all-reduce | flops 16384 | bytes 98304 | tf_op jit(solution)/shard_map/psum | solution.py:48
  254.1 0.0 copy-start.1
  254.5 25.7 %all_to_all.12 = bf16[32,16,1024]{2,1,0:T(8,128)(2,1)S(1)} all-to-all(bf16[32,16,1024]{2,1,0:T(8,128)(2,1)S(1)} %bitcast.9), channel_id=1, replica_groups=mesh['wide'=32,'narrow'=4] {'wide'}, dimensions={0} | all-to-all | bytes 2097152 | tf_op jit(solution)/shard_map/all_to_all | solution.py:11
  280.2 0.0 copy-done.1
  280.2 4.1 %convolution_convert_fusion = bf16[2048,1024]{1,0:T(8,128)(2,1)} fusion(bf16[512,1024]{1,0:T(8,128)(2,1)S(1)} %bitcast.10, f32[2048,512]{1,0:T(8,128)S(1)} %copy-done.1, f32[2048]{0:T(1024)S(1)} %get-tuple-element.5, f32[2048]{0:T(1024)S(1)} %get-tuple-element.7), kind=kOutput, calls=%fused_computation.3 | convolution fusion | flops 2152726528 | bytes 9453568 | tf_op jit(solution)/shard_map/dot_general | solution.py:50
  (34 shorter events, 0.2 us)
Async XLA Ops:
  6.5 1.2 copy-start
  6.5 157.6 %reduce-scatter.2.cloned.1.call-start = ((), (), s32[]{:S(2)}) async-start(), calls=%async_computation.2 | async-start | bytes 2162688 | tf_op jit(solution)/shard_map/reduce_scatter | solution.py:28
  90.2 143.2 %all-reduce.2.cloned.1.call-start = ((), (), s32[]{:S(2)}) async-start(), calls=%async_computation.3 | async-start | bytes 131072 | tf_op jit(solution)/shard_map/psum | solution.py:36
  254.1 26.1 %copy-start.1 = (f32[2048,512]{1,0:T(8,128)S(1)}, f32[2048,512]{1,0:T(8,128)}, u32[]{:S(2)}) copy-start(f32[2048,512]{1,0:T(8,128)} %get-tuple-element.9) | copy-start | bytes 12582916
Sparse Core Ops, SparseCore 0:
  90.3 73.7 reduce-scatter.1
  166.4 40.0 all-reduce.1
